TPU v7x, 32 devices: a whole 2x2x4 slice. The times are simulated.
32 devices in a mesh: fsdp: 16 (over z, x, core), rep: 2 (over y).
Axes of the slice: x: 2, y: 2, z: 4, core: 2. Of those that a mesh axis runs over, the one named last changes fastest.
Arguments:
- layer_input: bfloat16 [128, 256, 768], P(('fsdp', 'rep')), may hold values from -6 to 6
- slot_valid: int32 [128, 256], P(('fsdp', 'rep')), may hold values from 0 to 1, as said below
- projections: bfloat16 [3, 768, 768], P(None, 'fsdp'), may hold values from -0.21875 to 0.21875
- out_weight: bfloat16 [768, 768], P('fsdp'), may hold values from -1.25 to 1.25
- vectors: bfloat16 [8, 768], P(None, 'fsdp'), may hold values from -2 to 2
- up_weight: bfloat16 [768, 3072], P('fsdp'), may hold values from -0.21875 to 0.21875
- up_bias: bfloat16 [3072], P('fsdp'), may hold values from -3 to 3
- down_weight: bfloat16 [3072, 768], P('fsdp'), may hold values from -0.109375 to 0.109375
- cotangent: bfloat16 [128, 256, 768], P(('fsdp', 'rep')), may hold values from -6 to 6
Outputs:
- output: bfloat16 [128, 256, 768], P(('fsdp', 'rep'))
- grad_input: bfloat16 [128, 256, 768], P(('fsdp', 'rep'))
- grad_projections: float32 [3, 768, 768], P(None, 'fsdp')
- grad_out_weight: float32 [768, 768], P('fsdp')
- grad_vectors: float32 [8, 768], P(None, 'fsdp')
- grad_up_weight: float32 [768, 3072], P('fsdp')
- grad_up_bias: float32 [3072], P('fsdp')
- grad_down_weight: float32 [3072, 768], P('fsdp')
Inputs may be any that keep to these rules, and one draw needn't show every extreme that they name: `slot_valid`: in each sequence the first 128 slots are 1; of the next 128 slots the first k are 1 and the rest 0, with k from 10 to 100, both of which occur in every draw.
All inputs are finite; a program needn't handle non-finite values.
Results may differ from a plain program's by a relative error of at most 0.02.
Values may be sent and summed in bfloat16 or wider, within the bound.
No kernel may reach another device: no remote copies, remote signals or barrier semaphores. Data moves between devices by JAX's collectives and lax.ppermute only.
A program may use at most 192 MiB of HBM per device.

v0:
```python
from functools import partial
import jax
import jax.numpy as jnp
from jax import lax
from jax.sharding import PartitionSpec as P

HEADS = 12
HD = 64
EPSILON = 1e-12
MASKED = -1e30


def normalize(values, gain, shift):
    centered = values - jnp.mean(values, axis=-1, keepdims=True)
    spread = jnp.mean(centered * centered, axis=-1, keepdims=True)
    return centered * lax.rsqrt(spread + EPSILON) * gain + shift


def column_sum(values):
    return jnp.sum(values.astype(jnp.float32), axis=0)


def body(
    layer_input,
    slot_valid,
    projections,
    out_weight,
    vectors,
    up_weight,
    up_bias,
    down_weight,
    cotangent,
):
    seq_count, slot_count, model_width = layer_input.shape
    score_scale = HD ** (-0.5)
    shape_heads = (seq_count, slot_count, HEADS, HD)
    qkv_all, out_all, vec_all = (
        lax.all_gather(projections, "fsdp", axis=1, tiled=True),
        lax.all_gather(out_weight, "fsdp", axis=0, tiled=True),
        lax.all_gather(vectors, "fsdp", axis=1, tiled=True),
    )
    in_all, bias_in_all, down_all = (
        lax.all_gather(up_weight, "fsdp", axis=0, tiled=True),
        lax.all_gather(up_bias, "fsdp", axis=0, tiled=True),
        lax.all_gather(down_weight, "fsdp", axis=0, tiled=True),
    )
    bias_q, bias_v, bias_out, gain_one, shift_one, bias_down, gain_two, shift_two = vec_all.astype(
        jnp.float32
    )
    token_rows = layer_input.reshape(-1, model_width)
    query_low = (
        jnp.dot(token_rows, qkv_all[0], preferred_element_type=jnp.float32) + bias_q
    ).astype(jnp.bfloat16)
    key_low = jnp.dot(token_rows, qkv_all[1], preferred_element_type=jnp.float32).astype(
        jnp.bfloat16
    )
    value_low = (
        jnp.dot(token_rows, qkv_all[2], preferred_element_type=jnp.float32) + bias_v
    ).astype(jnp.bfloat16)
    query_heads = query_low.reshape(shape_heads)
    key_heads = key_low.reshape(shape_heads)
    value_heads = value_low.reshape(shape_heads)
    key_live = (slot_valid > 0)[:, None, None, :]

    def scores_of():
        raw = (
            jnp.einsum(
                "nqhe,nkhe->nhqk", query_heads, key_heads, preferred_element_type=jnp.float32
            )
            * score_scale
        )
        return jnp.where(key_live, raw, MASKED)

    scores = scores_of()
    row_max = jnp.max(scores, axis=-1, keepdims=True)
    exp_scores = jnp.exp(scores - row_max)
    exp_total = jnp.sum(exp_scores, axis=-1, keepdims=True)
    log_total = row_max + jnp.log(exp_total)
    probs_low = (exp_scores / exp_total).astype(jnp.bfloat16)
    context = jnp.einsum(
        "nhqk,nkhe->nqhe", probs_low, value_heads, preferred_element_type=jnp.float32
    )
    context = context.reshape(-1, model_width).astype(jnp.bfloat16)
    first_sum = (
        token_rows.astype(jnp.float32)
        + jnp.dot(context, out_all, preferred_element_type=jnp.float32)
        + bias_out
    )
    normed, norm_one_back = jax.vjp(normalize, first_sum, gain_one, shift_one)
    normed_low = normed.astype(jnp.bfloat16)
    hidden_pre = jnp.dot(
        normed_low, in_all, preferred_element_type=jnp.float32
    ) + bias_in_all.astype(jnp.float32)
    activated, gelu_back = jax.vjp(partial(jax.nn.gelu, approximate=False), hidden_pre)
    active_low = activated.astype(jnp.bfloat16)
    second_sum = (
        normed + jnp.dot(active_low, down_all, preferred_element_type=jnp.float32) + bias_down
    )
    normed_two, norm_two_back = jax.vjp(normalize, second_sum, gain_two, shift_two)
    row_live = slot_valid.reshape(-1, 1).astype(jnp.float32)
    output = (normed_two * row_live).astype(jnp.bfloat16).reshape(layer_input.shape)
    grad_rows = cotangent.reshape(-1, model_width).astype(jnp.float32) * row_live
    grad_second, grad_gain_two, grad_shift_two = norm_two_back(grad_rows)
    grad_second_low = grad_second.astype(jnp.bfloat16)
    in_back, down_back = (
        lax.all_gather(up_weight, "fsdp", axis=0, tiled=True),
        lax.all_gather(down_weight, "fsdp", axis=0, tiled=True),
    )
    grad_down = jnp.dot(active_low.T, grad_second_low, preferred_element_type=jnp.float32)
    grad_bias_down = column_sum(grad_second_low)
    grad_active = jnp.dot(grad_second_low, down_back.T, preferred_element_type=jnp.float32)
    grad_hidden_low = gelu_back(grad_active)[0].astype(jnp.bfloat16)
    grad_up = jnp.dot(normed_low.T, grad_hidden_low, preferred_element_type=jnp.float32)
    grad_bias_up = column_sum(grad_hidden_low)
    grad_normed = grad_second_low.astype(jnp.float32) + jnp.dot(
        grad_hidden_low, in_back.T, preferred_element_type=jnp.float32
    )
    ffn_parts = (
        lax.psum_scatter(
            grad_up.astype(jnp.bfloat16), "fsdp", scatter_dimension=0, tiled=True
        ).astype(jnp.float32),
        lax.psum_scatter(
            grad_bias_up.astype(jnp.bfloat16), "fsdp", scatter_dimension=0, tiled=True
        ).astype(jnp.float32),
        lax.psum_scatter(
            grad_down.astype(jnp.bfloat16), "fsdp", scatter_dimension=0, tiled=True
        ).astype(jnp.float32),
    )
    ffn_parts = (
        lax.psum(ffn_parts[0].astype(jnp.bfloat16), "rep").astype(jnp.float32),
        lax.psum(ffn_parts[1].astype(jnp.bfloat16), "rep").astype(jnp.float32),
        lax.psum(ffn_parts[2].astype(jnp.bfloat16), "rep").astype(jnp.float32),
    )
    grad_first, grad_gain_one, grad_shift_one = norm_one_back(grad_normed)
    grad_first_low = grad_first.astype(jnp.bfloat16)
    qkv_back, out_back = (
        lax.all_gather(projections, "fsdp", axis=1, tiled=True),
        lax.all_gather(out_weight, "fsdp", axis=0, tiled=True),
    )
    grad_out = jnp.dot(context.T, grad_first_low, preferred_element_type=jnp.float32)
    grad_bias_out = column_sum(grad_first_low)
    grad_context = (
        jnp.dot(grad_first_low, out_back.T, preferred_element_type=jnp.float32)
        .astype(jnp.bfloat16)
        .reshape(shape_heads)
    )
    weights_soft = jnp.exp(scores_of() - log_total)
    probs_again = weights_soft.astype(jnp.bfloat16)
    grad_value = jnp.einsum(
        "nhqk,nqhe->nkhe", probs_again, grad_context, preferred_element_type=jnp.float32
    )
    grad_value = grad_value.reshape(-1, model_width).astype(jnp.bfloat16)
    grad_probs = jnp.einsum(
        "nqhe,nkhe->nhqk", grad_context, value_heads, preferred_element_type=jnp.float32
    )
    grad_scores = (
        weights_soft * (grad_probs - jnp.sum(weights_soft * grad_probs, axis=-1, keepdims=True))
    ).astype(jnp.bfloat16)
    grad_query = (
        jnp.einsum("nhqk,nkhe->nqhe", grad_scores, key_heads, preferred_element_type=jnp.float32)
        * score_scale
    )
    grad_query = grad_query.reshape(-1, model_width).astype(jnp.bfloat16)
    grad_key = (
        jnp.einsum("nhqk,nqhe->nkhe", grad_scores, query_heads, preferred_element_type=jnp.float32)
        * score_scale
    )
    grad_key = grad_key.reshape(-1, model_width).astype(jnp.bfloat16)
    grad_stack = jnp.stack(
        [
            jnp.dot(token_rows.T, grad_query, preferred_element_type=jnp.float32),
            jnp.dot(token_rows.T, grad_key, preferred_element_type=jnp.float32),
            jnp.dot(token_rows.T, grad_value, preferred_element_type=jnp.float32),
        ]
    )
    grad_vectors = jnp.stack(
        [
            column_sum(grad_query),
            column_sum(grad_value),
            grad_bias_out,
            grad_gain_one,
            grad_shift_one,
            grad_bias_down,
            grad_gain_two,
            grad_shift_two,
        ]
    )
    grad_total = grad_first_low.astype(jnp.float32)
    grad_total = grad_total + jnp.dot(grad_query, qkv_back[0].T, preferred_element_type=jnp.float32)
    grad_total = grad_total + jnp.dot(grad_key, qkv_back[1].T, preferred_element_type=jnp.float32)
    grad_total = grad_total + jnp.dot(grad_value, qkv_back[2].T, preferred_element_type=jnp.float32)
    grad_input = grad_total.astype(jnp.bfloat16).reshape(layer_input.shape)
    attn_parts = (
        lax.psum_scatter(
            grad_stack.astype(jnp.bfloat16), "fsdp", scatter_dimension=1, tiled=True
        ).astype(jnp.float32),
        lax.psum_scatter(
            grad_out.astype(jnp.bfloat16), "fsdp", scatter_dimension=0, tiled=True
        ).astype(jnp.float32),
        lax.psum_scatter(
            grad_vectors.astype(jnp.bfloat16), "fsdp", scatter_dimension=1, tiled=True
        ).astype(jnp.float32),
    )
    attn_parts = (
        lax.psum(attn_parts[0].astype(jnp.bfloat16), "rep").astype(jnp.float32),
        lax.psum(attn_parts[1].astype(jnp.bfloat16), "rep").astype(jnp.float32),
        lax.psum(attn_parts[2].astype(jnp.bfloat16), "rep").astype(jnp.float32),
    )
    return (
        output,
        grad_input,
        attn_parts[0],
        attn_parts[1],
        attn_parts[2],
        ffn_parts[0],
        ffn_parts[1],
        ffn_parts[2],
    )


def solution(mesh):
    placed = (
        P(("fsdp", "rep"), None, None),
        P(("fsdp", "rep"), None),
        P(None, "fsdp", None),
        P("fsdp", None),
        P(None, "fsdp"),
        P("fsdp", None),
        P("fsdp"),
        P("fsdp", None),
        P(("fsdp", "rep"), None, None),
    )
    return jax.shard_map(
        body,
        mesh=mesh,
        in_specs=placed,
        out_specs=(
            P(("fsdp", "rep"), None, None),
            P(("fsdp", "rep"), None, None),
            P(None, "fsdp", None),
            P("fsdp", None),
            P(None, "fsdp"),
            P("fsdp", None),
            P("fsdp"),
            P("fsdp", None),
        ),
        check_vma=False,
    )
```

profile of v0, /device:TPU:0, one launch (start us, length us, event | category | flops | bytes accessed | tf_op | source)
XLA Modules:
  0.0 753.9 jit_solution(702271938507066873)
XLA Ops:
  12.0 23.5 %all-gather = bf16[16,48,8]{1,2,0:T(8,128)(2,1)S(1)} all-gather(bf16[1,48,8]{1,2,0:T(8,128)(2,1)} %bitcast.138), channel_id=1, replica_groups=mesh['fsdp'=16,'rep'=2] {'fsdp'}, dimensions={0}, use_global_device_ids=true | all-gather | bytes 13056 | tf_op jit(solution)/shard_map/all_gather | solution.py:40
  38.5 31.3 %all-reduce = bf16[3072]{0:T(1024)(128)(2,1)S(1)} all-reduce(bf16[3072]{0:T(1024)(128)(2,1)S(1)} %dynamic-update-slice), channel_id=1, replica_groups=mesh['fsdp'=16,'rep'=2] {'fsdp'}, use_global_device_ids=true, to_apply=%add | all-reduce | flops 3072 | bytes 12288
  83.2 4.8 add_convert_fusion.5
  108.5 4.0 fusion.56
  114.1 40.7 %all-gather.10.cloned.1.call-done = bf16[768,3072]{1,0:T(8,128)(2,1)} async-done(((bf16[48,3072]{1,0:T(8,128)(2,1)}), bf16[768,3072]{1,0:T(8,128)(2,1)}) %all-gather.10.cloned.1.call-update) | async-done | bytes 4718608 | tf_op jit(solution)/shard_map/all_gather | solution.py:43
  154.8 36.1 %multiply_convert_fusion.1 = (bf16[1024,3072]{1,0:T(8,128)(2,1)}, f32[1024,3072]{1,0:T(8,128)}, f32[1024,3072]{1,0:T(8,128)}) fusion(f32[3072]{0:T(1024)S(1)} %convert_element_type.182, bf16[768,3072]{1,0:T(8,128)(2,1)} %all-gather.10.cloned.1.call-done, f32[1024,768]{1,0:T(8,128)S(1)} %get-tuple-element.69, f32[768]{0:T(1024)S(1)} %get-tuple-element.40, ...), kind=kOutput, calls=%fused_computation.6 | convolution fusion | flops 5043388416 | bytes 39348224 | tf_op jit(solution)/shard_map/dot_general | solution.py:91
  190.9 17.7 %all-gather.12.cloned.1.call-done = bf16[3072,768]{1,0:T(8,128)(2,1)} async-done(((bf16[192,768]{1,0:T(8,128)(2,1)}), bf16[3072,768]{1,0:T(8,128)(2,1)}) %all-gather.12.cloned.1.call-update) | async-done | bytes 4718608 | tf_op jit(solution)/shard_map/all_gather | solution.py:45
  208.7 8.8 %fusion.57 = (f32[1024]{0:T(1024)S(1)}, f32[1024,768]{1,0:T(8,128)S(1)}) fusion(f32[768]{0:T(1024)S(1)} %get-tuple-element.39, bf16[1024,3072]{1,0:T(8,128)(2,1)} %get-tuple-element.59, bf16[3072,768]{1,0:T(8,128)(2,1)} %all-gather.12.cloned.1.call-done, f32[768]{0:T(1024)S(1)} %get-tuple-element.40, f32[768]{0:T(1024)S(1)} %get-tuple-element.41, ...), kind=kOutput, calls=%fused_computation.120 | convolution fusion | flops 4837342208 | bytes 17323008 | tf_op jit(solution)/shard_map/dot_general | solution.py:97
  223.7 17.3 %fusion.60 = (bf16[3072]{0:T(1024)(128)(2,1)S(1)}, bf16[1024,3072]{1,0:T(8,128)(2,1)}) fusion(f32[1024,3072]{1,0:T(8,128)} %get-tuple-element.60, bf16[1024,768]{1,0:T(8,128)(2,1)S(1)} %get-tuple-element.52, bf16[3072,768]{1,0:T(8,128)(2,1)} %all-gather.12.cloned.1.call-done, f32[1024,3072]{1,0:T(8,128)} %get-tuple-element.70, ...), kind=kOutput, calls=%fused_computation.123 | convolution fusion | flops 4882166784 | bytes 37767168 | tf_op jit(solution)/shard_map/dot_general | solution.py:111
  241.0 9.7 %multiply_reduce_fusion.3 = (bf16[768]{0:T(1024)(128)(2,1)S(1)}, f32[1024]{0:T(1024)S(1)}, bf16[768]{0:T(1024)(128)(2,1)S(1)}, f32[1024,768]{1,0:T(8,128)S(1)}) fusion(f32[1024,768]{1,0:T(8,128)S(1)} %copy-done.7, f32[1024]{0:T(1024)S(1)} %fusion.40, f32[1024]{0:T(1024)S(1)} %broadcast_multiply_fusion.1, f32[768]{0:T(1024)S(1)} %get-tuple-element.41, ...), kind=kOutput, calls=%fused_computation.37 | convolution fusion | flops 4839699456 | bytes 18892800 | tf_op jit(solution)/shard_map/dot_general | solution.py:115
  262.8 8.6 %multiply_reduce_fusion = (f32[4,12,256]{2,1,0:T(8,128)S(1)}, f32[4,12,256,256]{2,3,1,0:T(8,128)S(1)}) fusion(f32[4,12,256]{2,1,0:T(8,128)S(1)} %copy-done.20, f32[4,12,256,256]{2,3,1,0:T(8,128)} %copy-done, pred[4,256]{1,0:T(4,128)(4,1)S(1)} %copy-done.22, bf16[4,256,12,64]{1,0,3,2:T(4,128)(2,1)S(1)} %copy-done.9, bf16[4,256,12,64]{1,0,3,2:T(4,128)(2,1)} %reshape.155), kind=kOutput, calls=%fused_computation.3 | convolution fusion | flops 418369536 | bytes 28410880 | tf_op jit(solution)/shard_map/nqhe,nkhe->nhqk/dot_general | solution.py:153
  271.4 8.0 %multiply_convert_fusion = bf16[4,12,256,256]{2,3,1,0:T(8,128)(2,1)S(1)} fusion(f32[4,12,256,256]{2,3,1,0:T(8,128)S(1)} %get-tuple-element.75, f32[4,12,256]{2,1,0:T(8,128)S(1)} %get-tuple-element.74, f32[4,12,256]{2,1,0:T(8,128)S(1)} %copy-done.20, f32[4,12,256,256]{2,3,1,0:T(8,128)} %copy-done, pred[4,256]{1,0:T(4,128)(4,1)S(1)} %copy-done.22), kind=kLoop, calls=%fused_computation.2 | loop fusion | flops 18874368 | bytes 31556608 | tf_op jit(solution)/shard_map/convert_element_type | solution.py:158
  300.3 8.1 %copy.73 = bf16[3,768,768]{2,0,1:T(4,128)(2,1)} copy(bf16[3,768,768]{1,2,0:T(8,128)(2,1)} %pad_maximum_fusion) | data formatting | bytes 7077888 | tf_op jit(solution)/shard_map/stack | solution.py:169
  313.7 10.7 %convolution_convert_fusion.1 = bf16[768,3072]{1,0:T(8,128)(2,1)} fusion(bf16[1024,3072]{1,0:T(8,128)(2,1)} %get-tuple-element.81, f32[1024,768]{1,0:T(8,128)} %copy-done.6, f32[768]{0:T(1024)S(1)} %get-tuple-element.40, f32[768]{0:T(1024)S(1)} %get-tuple-element.41, f32[1024]{0:T(1024)S(1)} %fusion.40, f32[1024]{0:T(1024)S(1)} %broadcast_multiply_fusion.1), kind=kOutput, calls=%fused_computation.30 | convolution fusion | flops 4838129664 | bytes 14170112 | tf_op jit(solution)/shard_map/dot_general | solution.py:113
  324.5 9.3 %convolution_convert_fusion = bf16[3072,768]{1,0:T(8,128)(2,1)} fusion(bf16[1024,3072]{1,0:T(8,128)(2,1)} %get-tuple-element.59, bf16[1024,768]{1,0:T(8,128)(2,1)} %copy-done.16), kind=kOutput, calls=%fused_computation.29 | convolution fusion | flops 4834197504 | bytes 12582912 | tf_op jit(solution)/shard_map/dot_general | solution.py:109
  337.2 32.7 %all-reduce.2 = bf16[3072]{0:T(1024)(128)(2,1)S(1)} all-reduce(bf16[3072]{0:T(1024)(128)(2,1)S(1)} %get-tuple-element.80), channel_id=6, replica_groups=mesh['fsdp'=16,'rep'=2] {'fsdp'}, use_global_device_ids=true, to_apply=%region_28.29.clone | all-reduce | flops 3072 | bytes 12288
  370.1 5.1 fusion.39
  375.1 49.2 %all-reduce.8.cloned.1.call-done = bf16[3,768,768]{2,0,1:T(4,128)(2,1)} async-done(((bf16[3,768,768]{2,0,1:T(4,128)(2,1)}), bf16[3,768,768]{2,0,1:T(4,128)(2,1)}) %all-reduce.8.cloned.1.call-update) | async-done | bytes 3538960
  426.1 59.6 %reduce-scatter.7.cloned.1.call-done = bf16[48,768]{1,0:T(8,128)(2,1)} async-done(((bf16[768,768]{1,0:T(8,128)(2,1)}), bf16[48,768]{1,0:T(8,128)(2,1)}) %reduce-scatter.7.cloned.1.call-update) | async-done | bytes 73744 | tf_op jit(solution)/shard_map/reduce_scatter | solution.py:197
  485.7 78.6 %reduce-scatter.9.cloned.1.call-done = bf16[48,3072]{1,0:T(8,128)(2,1)} async-done(((bf16[768,3072]{1,0:T(8,128)(2,1)}), bf16[48,3072]{1,0:T(8,128)(2,1)}) %reduce-scatter.9.cloned.1.call-update) | async-done | bytes 294928 | tf_op jit(solution)/shard_map/reduce_scatter | solution.py:119
  564.3 78.7 %reduce-scatter.11.cloned.1.call-done = bf16[192,768]{1,0:T(8,128)(2,1)} async-done(((bf16[3072,768]{1,0:T(8,128)(2,1)}), bf16[192,768]{1,0:T(8,128)(2,1)}) %reduce-scatter.11.cloned.1.call-update) | async-done | bytes 294928 | tf_op jit(solution)/shard_map/reduce_scatter | solution.py:125
  649.8 49.6 %reduce-scatter.13.cloned.1.call-done = bf16[48,8]{1,0:T(8,128)(2,1)} async-done(((bf16[768,8]{1,0:T(8,128)(2,1)}), bf16[48,8]{1,0:T(8,128)(2,1)}) %reduce-scatter.13.cloned.1.call-update) | async-done | bytes 784
  700.3 4.9 all-reduce.3
  706.3 33.3 %all-reduce.10.cloned.1.call-done = (bf16[3,48,768]{2,0,1:T(4,128)(2,1)}, bf16[48,768]{1,0:T(8,128)(2,1)}, bf16[48,3072]{1,0:T(8,128)(2,1)}, bf16[192,768]{1,0:T(8,128)(2,1)}) async-done(((bf16[3,48,768]{2,0,1:T(4,128)(2,1)}, bf16[48,768]{1,0:T(8,128)(2,1)}, bf16[48,3072]{1,0:T(8,128)(2,1)}, bf16[192,768]{1,0:T(8,128)(2,1)}), (bf16[3,48,768]{2,0,1:T(4,128)(2,1)}, bf16[48,768]{1,0:T(8,128)(2,1)}, ...) | async-done | bytes 884752 | tf_op jit(solution)/shard_map/psum | solution.py:205
  (159 shorter events, 106.3 us)
Async XLA Ops:
  7.2 62.7 %all-gather.6.cloned.1.call-start = ((), (), s32[]{:S(2)}) async-start(), calls=%async_computation.4 | async-start | bytes 3760128 | tf_op jit(solution)/shard_map/all_gather | solution.py:38
  7.9 100.6 %all-gather.8.cloned.1.call-start = ((), (), s32[]{:S(2)}) async-start(), calls=%async_computation.5 | async-start | bytes 1253376 | tf_op jit(solution)/shard_map/all_gather | solution.py:39
  8.6 146.2 %all-gather.10.cloned.1.call-start = ((), (), s32[]{:S(2)}) async-start(), calls=%async_computation.6 | async-start | bytes 5013504 | tf_op jit(solution)/shard_map/all_gather | solution.py:43
  9.4 199.3 %all-gather.12.cloned.1.call-start = ((), (), s32[]{:S(2)}) async-start(), calls=%async_computation.7 | async-start | bytes 5013504 | tf_op jit(solution)/shard_map/all_gather | solution.py:45
  10.0 414.4 %all-reduce.8.cloned.1.call-start = ((), (), s32[]{:S(2)}) async-start(), calls=%async_computation.12 | async-start | bytes 9437184
  10.7 90.7 %copy-start.21 = (pred[4,256]{1,0:T(4,128)(4,1)}, pred[4,256]{1,0:T(4,128)(4,1)S(1)}, u32[]{:S(2)}) copy-start(pred[4,256]{1,0:T(4,128)(4,1)S(1)} %broadcast_compare_fusion) | copy-start | bytes 3076
  75.0 19.5 %copy-start.4 = (bf16[4,256,12,64]{1,0,3,2:T(4,128)(2,1)}, bf16[4,256,12,64]{1,0,3,2:T(4,128)(2,1)S(1)}, u32[]{:S(2)}) copy-start(bf16[4,256,12,64]{1,0,3,2:T(4,128)(2,1)S(1)} %reshape.153) | copy-start | bytes 4718596
  83.2 11.3 %copy-start.1 = (bf16[4,256,12,64]{1,0,3,2:T(4,128)(2,1)}, bf16[4,256,12,64]{1,0,3,2:T(4,128)(2,1)S(1)}, u32[]{:S(2)}) copy-start(bf16[4,256,12,64]{1,0,3,2:T(4,128)(2,1)S(1)} %reshape.152) | copy-start | bytes 4718596
  97.6 4.8 copy-start
  112.5 96.1 %copy-start.6 = (f32[1024,768]{1,0:T(8,128)}, f32[1024,768]{1,0:T(8,128)S(1)}, u32[]{:S(2)}) copy-start(f32[1024,768]{1,0:T(8,128)S(1)} %get-tuple-element.69) | copy-start | bytes 9437188
  223.6 17.3 %copy-start.16 = (bf16[1024,768]{1,0:T(8,128)(2,1)}, bf16[1024,768]{1,0:T(8,128)(2,1)S(1)}, u32[]{:S(2)}) copy-start(bf16[1024,768]{1,0:T(8,128)(2,1)S(1)} %get-tuple-element.52) | copy-start | bytes 4718596
  223.6 17.3 %copy-start.7 = (f32[1024,768]{1,0:T(8,128)S(1)}, f32[1024,768]{1,0:T(8,128)}, u32[]{:S(2)}) copy-start(f32[1024,768]{1,0:T(8,128)} %copy-done.6) | copy-start | bytes 9437188
  256.2 6.6 copy-start.9
  256.2 6.6 copy-start.20
  256.2 6.6 copy-start.22
  271.4 8.1 %copy-start.2 = (bf16[4,256,12,64]{1,0,3,2:T(4,128)(2,1)S(1)}, bf16[4,256,12,64]{1,0,3,2:T(4,128)(2,1)}, u32[]{:S(2)}) copy-start(bf16[4,256,12,64]{1,0,3,2:T(4,128)(2,1)} %copy-done.1) | copy-start | bytes 4718596
  290.4 5.0 copy-start.19
  292.0 4.8 copy-start.17
  308.5 177.2 %reduce-scatter.7.cloned.1.call-start = ((), (), s32[]{:S(2)}) async-start(), calls=%async_computation.8 | async-start | bytes 1253376 | tf_op jit(solution)/shard_map/reduce_scatter | solution.py:197
  313.7 250.6 %reduce-scatter.9.cloned.1.call-start = ((), (), s32[]{:S(2)}) async-start(), calls=%async_computation.9 | async-start | bytes 5013504 | tf_op jit(solution)/shard_map/reduce_scatter | solution.py:119
  324.4 318.5 %reduce-scatter.11.cloned.1.call-start = ((), (), s32[]{:S(2)}) async-start(), calls=%async_computation.10 | async-start | bytes 5013504 | tf_op jit(solution)/shard_map/reduce_scatter | solution.py:125
  333.8 365.7 %reduce-scatter.13.cloned.1.call-start = ((), (), s32[]{:S(2)}) async-start(), calls=%async_computation.11 | async-start | bytes 208896
  369.9 369.7 %all-reduce.10.cloned.1.call-start = ((), (), s32[]{:S(2)}) async-start(), calls=%async_computation.13 | async-start | bytes 1916928 | tf_op jit(solution)/shard_map/psum | solution.py:205
  370.1 272.9 %copy-start.18 = (bf16[96,8,4,256]{3,1,2,0:T(8,128)(2,1)S(1)}, bf16[96,8,4,256]{3,1,2,0:T(8,128)(2,1)}, u32[]{:S(2)}) copy-start(bf16[96,8,4,256]{3,1,2,0:T(8,128)(2,1)} %copy-done.17) | copy-start | bytes 4718596
  (15 other events, 36.6 us)
Sparse Core Ops, SparseCore 0:
  10.3 50.7 all-gather.5
  63.3 37.0 all-gather.7
  102.8 51.9 all-gather.9
  156.9 51.6 all-gather.11
  308.6 115.6 all-reduce.7
  427.8 57.8 reduce-scatter.6
  489.6 74.6 reduce-scatter.8
  568.2 74.7 reduce-scatter.10
  647.0 52.4 reduce-scatter.12
  702.4 37.1 all-reduce.9
where the time goes:
time: 765 us; the launch traced here: 754 us
  waiting for transfers between devices  410 us (54%)
  matrix products  152 us (20%)
  blocking collectives  92.3 us (12%)
  local copies, waits for them, and re-layouts  50.5 us (7%)
  other arithmetic  31.3 us (4%)
  between operations  17.2 us (2%)
    unnamed x12, waiting for transfers between devices  102 us
    reduce_scatter x1, waiting for transfers between devices, body(): lax.psum_scatter(grad_down.astype(jnp.bfloat16), 'fsdp', scatter_dimensio...  78.7 us
    reduce_scatter x1, waiting for transfers between devices, body(): lax.psum_scatter(grad_up.astype(jnp.bfloat16), 'fsdp', scatter_dimension=...  78.6 us
    unnamed x2, blocking collectives  64 us
    reduce_scatter x1, waiting for transfers between devices, body(): lax.psum_scatter(grad_out.astype(jnp.bfloat16), 'fsdp', scatter_dimension...  59.6 us
    all_gather x1, waiting for transfers between devices, body(): lax.all_gather(up_weight, 'fsdp', axis=0, tiled=True)  40.7 us
    dot_general x1, matrix products, body(): jnp.dot(normed_low, in_all, preferred_element_type=jnp.float32)  36.1 us
    psum x1, waiting for transfers between devices, body(): lax.psum(attn_parts[0].astype(jnp.bfloat16), 'rep').astype(jnp.float32)  33.3 us
  transfers between devices with their start and end apart: 10, of which 8 were waited for; matrix products, arithmetic and copies ran while one was open for 17% of the time, Pallas kernels for 0%

commit v1 on v0

--- a/solution.py
+++ b/solution.py
@@ -1,13 +1,23 @@
+import functools
 from functools import partial
 import jax
 import jax.numpy as jnp
 from jax import lax
 from jax.sharding import PartitionSpec as P
+from jax.lax import all_gather
 
 HEADS = 12
 HD = 64
 EPSILON = 1e-12
 MASKED = -1e30
+
+
+def advance_heads_by_axis(view, axis_tag):
+    all_rows = all_gather(view, axis_tag)
+    return jnp.sum(all_rows, axis=0)
+
+
+routes_all_take = functools.partial(advance_heads_by_axis, axis_tag="rep")
 
 
 def normalize(values, gain, shift):
@@ -202,7 +212,7 @@
         ).astype(jnp.float32),
     )
     attn_parts = (
-        lax.psum(attn_parts[0].astype(jnp.bfloat16), "rep").astype(jnp.float32),
+        routes_all_take(attn_parts[0].astype(jnp.bfloat16)).astype(jnp.float32),
         lax.psum(attn_parts[1].astype(jnp.bfloat16), "rep").astype(jnp.float32),
         lax.psum(attn_parts[2].astype(jnp.bfloat16), "rep").astype(jnp.float32),
     )

time: 765 us -> 704 us (0.920)
  waiting for transfers between devices: 410 us -> 345 us
  local copies, waits for them, and re-layouts: 50.5 us -> 42.8 us
    unnamed x12, waiting for transfers between devices: 102 us -> 166 us
    reduce_scatter x1, waiting for transfers between devices: 78.6 us -> 16.9 us  [body(): lax.psum_scatter(grad_up.astype(jnp.bfloat16), 'fsdp', scatter_dimension=...]
    reduce_scatter x1, waiting for transfers between devices: 59.6 us -> 0.01 us  [body(): lax.psum_scatter(grad_out.astype(jnp.bfloat16), 'fsdp', scatter_dimension...]
    psum x1, waiting for transfers between devices: 33.3 us -> 24.4 us  [body(): lax.psum(attn_parts[1].astype(jnp.bfloat16), 'rep').astype(jnp.float32)]
    unnamed x71 -> x76, local copies, waits for them, and re-layouts: 17.6 us -> 14 us
  transfers between devices with their start and end apart: 10 -> 10, of which waited for: 8 -> 7; matrix products, arithmetic and copies ran while one was open for 17% -> 25% of each run, Pallas kernels for 0% -> 0%
where the time goes in v1:
time: 704 us; the launch traced here: 693 us
  waiting for transfers between devices  345 us (49%)
  matrix products  157 us (22%)
  blocking collectives  99.1 us (14%)
  local copies, waits for them, and re-layouts  42.8 us (6%)
  other arithmetic  30.7 us (4%)
  between operations  17.3 us (2%)
    unnamed x12, waiting for transfers between devices  166 us
    reduce_scatter x1, waiting for transfers between devices, body(): lax.psum_scatter(grad_down.astype(jnp.bfloat16), 'fsdp', scatter_dimensio...  78.7 us
    unnamed x2, blocking collectives  63.8 us
    all_gather x1, waiting for transfers between devices, body(): lax.all_gather(up_weight, 'fsdp', axis=0, tiled=True)  41.7 us
    dot_general x1, matrix products, body(): jnp.dot(normed_low, in_all, preferred_element_type=jnp.float32)  36.1 us
    psum x1, waiting for transfers between devices, body(): lax.psum(attn_parts[1].astype(jnp.bfloat16), 'rep').astype(jnp.float32)  24.4 us
    all_gather x1, blocking collectives, body(): lax.all_gather(vectors, 'fsdp', axis=1, tiled=True)  23.5 us
    all_gather x1, waiting for transfers between devices, body(): lax.all_gather(down_weight, 'fsdp', axis=0, tiled=True)  17.7 us
  transfers between devices with their start and end apart: 10, of which 7 were waited for; matrix products, arithmetic and copies ran while one was open for 25% of the time, Pallas kernels for 0%

profile of v1, /device:TPU:0, one launch (start us, length us, event | category | flops | bytes accessed | tf_op | source)
XLA Modules:
  0.0 693.1 jit_solution(5215666654349846593)
XLA Ops:
  12.0 23.5 %all-gather.1 = bf16[16,48,8]{1,2,0:T(8,128)(2,1)S(1)} all-gather(bf16[1,48,8]{1,2,0:T(8,128)(2,1)} %bitcast.140), channel_id=1, replica_groups=mesh['fsdp'=16,'rep'=2] {'fsdp'}, dimensions={0}, use_global_device_ids=true | all-gather | bytes 13056 | tf_op jit(solution)/shard_map/all_gather | solution.py:50
  38.5 31.3 %all-reduce = bf16[3072]{0:T(1024)(128)(2,1)S(1)} all-reduce(bf16[3072]{0:T(1024)(128)(2,1)S(1)} %dynamic-update-slice), channel_id=1, replica_groups=mesh['fsdp'=16,'rep'=2] {'fsdp'}, use_global_device_ids=true, to_apply=%add | all-reduce | flops 3072 | bytes 12288
  83.2 4.8 add_convert_fusion.5
  113.1 41.7 %all-gather.11.cloned.1.call-done = bf16[768,3072]{1,0:T(8,128)(2,1)} async-done(((bf16[48,3072]{1,0:T(8,128)(2,1)}), bf16[768,3072]{1,0:T(8,128)(2,1)}) %all-gather.11.cloned.1.call-update) | async-done | bytes 4718608 | tf_op jit(solution)/shard_map/all_gather | solution.py:53
  154.8 36.1 %multiply_convert_fusion.1 = (bf16[1024,3072]{1,0:T(8,128)(2,1)}, f32[1024,3072]{1,0:T(8,128)}, f32[1024,3072]{1,0:T(8,128)}) fusion(f32[3072]{0:T(1024)S(1)} %convert_element_type.184, bf16[768,3072]{1,0:T(8,128)(2,1)} %all-gather.11.cloned.1.call-done, f32[1024,768]{1,0:T(8,128)S(1)} %get-tuple-element.52, f32[768]{0:T(1024)S(1)} %get-tuple-element.24, ...), kind=kOutput, calls=%fused_computation.6 | convolution fusion | flops 5043388416 | bytes 39348224 | tf_op jit(solution)/shard_map/dot_general | solution.py:101
  190.9 17.7 %all-gather.13.cloned.1.call-done = bf16[3072,768]{1,0:T(8,128)(2,1)} async-done(((bf16[192,768]{1,0:T(8,128)(2,1)}), bf16[3072,768]{1,0:T(8,128)(2,1)}) %all-gather.13.cloned.1.call-update) | async-done | bytes 4718608 | tf_op jit(solution)/shard_map/all_gather | solution.py:55
  208.6 8.8 %fusion.57 = (f32[1024]{0:T(1024)S(1)}, f32[1024,768]{1,0:T(8,128)S(1)}) fusion(f32[768]{0:T(1024)S(1)} %get-tuple-element.23, bf16[1024,3072]{1,0:T(8,128)(2,1)} %get-tuple-element.42, bf16[3072,768]{1,0:T(8,128)(2,1)} %all-gather.13.cloned.1.call-done, f32[768]{0:T(1024)S(1)} %get-tuple-element.24, f32[768]{0:T(1024)S(1)} %get-tuple-element.25, ...), kind=kOutput, calls=%fused_computation.120 | convolution fusion | flops 4837342208 | bytes 17323008 | tf_op jit(solution)/shard_map/dot_general | solution.py:107
  223.6 17.3 %fusion.60 = (bf16[3072]{0:T(1024)(128)(2,1)S(1)}, bf16[1024,3072]{1,0:T(8,128)(2,1)}) fusion(f32[1024,3072]{1,0:T(8,128)} %get-tuple-element.43, bf16[1024,768]{1,0:T(8,128)(2,1)S(1)} %get-tuple-element.35, bf16[3072,768]{1,0:T(8,128)(2,1)} %all-gather.13.cloned.1.call-done, f32[1024,3072]{1,0:T(8,128)} %get-tuple-element.53, ...), kind=kOutput, calls=%fused_computation.123 | convolution fusion | flops 4882166784 | bytes 37767168 | tf_op jit(solution)/shard_map/dot_general | solution.py:121
  241.0 9.7 %multiply_reduce_fusion.3 = (bf16[768]{0:T(1024)(128)(2,1)S(1)}, f32[1024]{0:T(1024)S(1)}, bf16[768]{0:T(1024)(128)(2,1)S(1)}, f32[1024,768]{1,0:T(8,128)S(1)}) fusion(f32[1024,768]{1,0:T(8,128)S(1)} %copy-done.7, f32[1024]{0:T(1024)S(1)} %fusion.40, f32[1024]{0:T(1024)S(1)} %broadcast_multiply_fusion.1, f32[768]{0:T(1024)S(1)} %get-tuple-element.25, ...), kind=kOutput, calls=%fused_computation.37 | convolution fusion | flops 4839699456 | bytes 18892800 | tf_op jit(solution)/shard_map/dot_general | solution.py:125
  256.3 10.4 %convolution_convert_fusion.1 = bf16[768,3072]{1,0:T(8,128)(2,1)} fusion(bf16[1024,3072]{1,0:T(8,128)(2,1)} %get-tuple-element.64, f32[1024,768]{1,0:T(8,128)} %copy-done.6, f32[768]{0:T(1024)S(1)} %get-tuple-element.24, f32[768]{0:T(1024)S(1)} %get-tuple-element.25, f32[1024]{0:T(1024)S(1)} %fusion.40, f32[1024]{0:T(1024)S(1)} %broadcast_multiply_fusion.1), kind=kOutput, calls=%fused_computation.30 | convolution fusion | flops 4838129664 | bytes 14170112 | tf_op jit(solution)/shard_map/dot_general | solution.py:123
  266.7 9.3 %convolution_convert_fusion = bf16[3072,768]{1,0:T(8,128)(2,1)} fusion(bf16[1024,3072]{1,0:T(8,128)(2,1)} %get-tuple-element.42, bf16[1024,768]{1,0:T(8,128)(2,1)} %copy-done.14), kind=kOutput, calls=%fused_computation.29 | convolution fusion | flops 4834197504 | bytes 12582912 | tf_op jit(solution)/shard_map/dot_general | solution.py:119
  284.7 7.8 %multiply_reduce_fusion = (f32[4,12,256]{2,1,0:T(8,128)S(1)}, f32[4,12,256,256]{2,3,1,0:T(8,128)S(1)}) fusion(f32[4,12,256]{2,1,0:T(8,128)S(1)} %log_add_fusion, f32[4,12,256,256]{2,3,1,0:T(8,128)} %copy-done, pred[4,256]{1,0:T(4,128)(4,1)S(1)} %copy-done.25, bf16[4,256,12,64]{1,0,3,2:T(4,128)(2,1)S(1)} %copy-done.9, bf16[4,256,12,64]{1,0,3,2:T(4,128)(2,1)S(1)} %reshape.155), kind=kOutput, calls=%fused_computation.3 | convolution fusion | flops 418369536 | bytes 28410880 | tf_op jit(solution)/shard_map/nqhe,nkhe->nhqk/dot_general | solution.py:163
  292.5 8.0 %multiply_convert_fusion = bf16[4,12,256,256]{2,3,1,0:T(8,128)(2,1)S(1)} fusion(f32[4,12,256,256]{2,3,1,0:T(8,128)S(1)} %get-tuple-element.58, f32[4,12,256]{2,1,0:T(8,128)S(1)} %get-tuple-element.57, f32[4,12,256]{2,1,0:T(8,128)S(1)} %log_add_fusion, f32[4,12,256,256]{2,3,1,0:T(8,128)} %copy-done, pred[4,256]{1,0:T(4,128)(4,1)S(1)} %copy-done.25), kind=kLoop, calls=%fused_computation.2 | loop fusion | flops 18874368 | bytes 31556608 | tf_op jit(solution)/shard_map/convert_element_type | solution.py:168
  326.3 5.7 copy.71
  333.5 32.5 %all-reduce.2 = bf16[3072]{0:T(1024)(128)(2,1)S(1)} all-reduce(bf16[3072]{0:T(1024)(128)(2,1)S(1)} %get-tuple-element.63), channel_id=7, replica_groups=mesh['fsdp'=16,'rep'=2] {'fsdp'}, use_global_device_ids=true, to_apply=%region_28.29.clone | all-reduce | flops 3072 | bytes 12288
  370.6 4.6 fusion.38
  375.1 16.9 %reduce-scatter.9.cloned.1.call-done = bf16[48,3072]{1,0:T(8,128)(2,1)} async-done(((bf16[768,3072]{1,0:T(8,128)(2,1)}), bf16[48,3072]{1,0:T(8,128)(2,1)}) %reduce-scatter.9.cloned.1.call-update) | async-done | bytes 294928 | tf_op jit(solution)/shard_map/reduce_scatter | solution.py:129
  392.0 78.7 %reduce-scatter.11.cloned.1.call-done = bf16[192,768]{1,0:T(8,128)(2,1)} async-done(((bf16[3072,768]{1,0:T(8,128)(2,1)}), bf16[192,768]{1,0:T(8,128)(2,1)}) %reduce-scatter.11.cloned.1.call-update) | async-done | bytes 294928 | tf_op jit(solution)/shard_map/reduce_scatter | solution.py:135
  470.8 5.9 add_convert_fusion.1
  476.6 50.6 %reduce-scatter.13.cloned.1.call-done = bf16[48,8]{1,0:T(8,128)(2,1)} async-done(((bf16[768,8]{1,0:T(8,128)(2,1)}), bf16[48,8]{1,0:T(8,128)(2,1)}) %reduce-scatter.13.cloned.1.call-update) | async-done | bytes 784
  528.0 4.9 all-reduce.3
  534.1 112.7 %all-reduce.8.cloned.1.call-done = bf16[3,768,768]{2,0,1:T(4,128)(2,1)} async-done(((bf16[3,768,768]{2,0,1:T(4,128)(2,1)}), bf16[3,768,768]{2,0,1:T(4,128)(2,1)}) %all-reduce.8.cloned.1.call-update) | async-done | bytes 3538960
  647.9 6.9 all-gather
  656.2 24.4 %all-reduce.10.cloned.1.call-done = (bf16[48,768]{1,0:T(8,128)(2,1)}, bf16[48,3072]{1,0:T(8,128)(2,1)}, bf16[192,768]{1,0:T(8,128)(2,1)}) async-done(((bf16[48,768]{1,0:T(8,128)(2,1)}, bf16[48,3072]{1,0:T(8,128)(2,1)}, bf16[192,768]{1,0:T(8,128)(2,1)}), (bf16[48,768]{1,0:T(8,128)(2,1)}, bf16[48,3072]{1,0:T(8,128)(2,1)}, bf16[192,768]{1,0:T(8,128)(2,1)})) %all-reduce.10.cloned.1.call-update) | async-done | bytes 663568 | tf_op jit(solution)/shard_map/psum | solution.py:216
  (167 shorter events, 105.5 us)
Async XLA Ops:
  7.2 62.7 %all-gather.7.cloned.1.call-start = ((), (), s32[]{:S(2)}) async-start(), calls=%async_computation.4 | async-start | bytes 3760128 | tf_op jit(solution)/shard_map/all_gather | solution.py:48
  7.9 100.6 %all-gather.9.cloned.1.call-start = ((), (), s32[]{:S(2)}) async-start(), calls=%async_computation.5 | async-start | bytes 1253376 | tf_op jit(solution)/shard_map/all_gather | solution.py:49
  8.6 146.1 %all-gather.11.cloned.1.call-start = ((), (), s32[]{:S(2)}) async-start(), calls=%async_computation.6 | async-start | bytes 5013504 | tf_op jit(solution)/shard_map/all_gather | solution.py:53
  9.4 199.3 %all-gather.13.cloned.1.call-start = ((), (), s32[]{:S(2)}) async-start(), calls=%async_computation.7 | async-start | bytes 5013504 | tf_op jit(solution)/shard_map/all_gather | solution.py:55
  10.0 365.2 %reduce-scatter.7.cloned.1.call-start = ((), (), s32[]{:S(2)}) async-start(), calls=%async_computation.8 | async-start | bytes 1253376 | tf_op jit(solution)/shard_map/reduce_scatter | solution.py:207
  10.7 90.8 %copy-start.24 = (pred[4,256]{1,0:T(4,128)(4,1)}, pred[4,256]{1,0:T(4,128)(4,1)S(1)}, u32[]{:S(2)}) copy-start(pred[4,256]{1,0:T(4,128)(4,1)S(1)} %broadcast_compare_fusion) | copy-start | bytes 3076
  75.0 19.5 %copy-start.4 = (bf16[4,256,12,64]{1,0,3,2:T(4,128)(2,1)}, bf16[4,256,12,64]{1,0,3,2:T(4,128)(2,1)S(1)}, u32[]{:S(2)}) copy-start(bf16[4,256,12,64]{1,0,3,2:T(4,128)(2,1)S(1)} %reshape.153) | copy-start | bytes 4718596
  83.2 11.3 %copy-start.1 = (bf16[4,256,12,64]{1,0,3,2:T(4,128)(2,1)}, bf16[4,256,12,64]{1,0,3,2:T(4,128)(2,1)S(1)}, u32[]{:S(2)}) copy-start(bf16[4,256,12,64]{1,0,3,2:T(4,128)(2,1)S(1)} %reshape.152) | copy-start | bytes 4718596
  112.6 96.1 %copy-start.6 = (f32[1024,768]{1,0:T(8,128)}, f32[1024,768]{1,0:T(8,128)S(1)}, u32[]{:S(2)}) copy-start(f32[1024,768]{1,0:T(8,128)S(1)} %get-tuple-element.52) | copy-start | bytes 9437188
  223.6 17.3 %copy-start.14 = (bf16[1024,768]{1,0:T(8,128)(2,1)}, bf16[1024,768]{1,0:T(8,128)(2,1)S(1)}, u32[]{:S(2)}) copy-start(bf16[1024,768]{1,0:T(8,128)(2,1)S(1)} %get-tuple-element.35) | copy-start | bytes 4718596
  223.6 17.3 %copy-start.7 = (f32[1024,768]{1,0:T(8,128)S(1)}, f32[1024,768]{1,0:T(8,128)}, u32[]{:S(2)}) copy-start(f32[1024,768]{1,0:T(8,128)} %copy-done.6) | copy-start | bytes 9437188
  252.5 24.6 %copy-start.10 = (bf16[1024,768]{1,0:T(8,128)(2,1)}, bf16[1024,768]{1,0:T(8,128)(2,1)S(1)}, u32[]{:S(2)}) copy-start(bf16[1024,768]{1,0:T(8,128)(2,1)S(1)} %get-tuple-element.37) | copy-start | bytes 4718596
  256.2 135.8 %reduce-scatter.9.cloned.1.call-start = ((), (), s32[]{:S(2)}) async-start(), calls=%async_computation.9 | async-start | bytes 5013504 | tf_op jit(solution)/shard_map/reduce_scatter | solution.py:129
  266.7 204.0 %reduce-scatter.11.cloned.1.call-start = ((), (), s32[]{:S(2)}) async-start(), calls=%async_computation.10 | async-start | bytes 5013504 | tf_op jit(solution)/shard_map/reduce_scatter | solution.py:135
  276.0 251.2 %reduce-scatter.13.cloned.1.call-start = ((), (), s32[]{:S(2)}) async-start(), calls=%async_computation.11 | async-start | bytes 208896
  292.5 8.1 %copy-start.2 = (bf16[4,256,12,64]{1,0,3,2:T(4,128)(2,1)S(1)}, bf16[4,256,12,64]{1,0,3,2:T(4,128)(2,1)}, u32[]{:S(2)}) copy-start(bf16[4,256,12,64]{1,0,3,2:T(4,128)(2,1)} %copy-done.1) | copy-start | bytes 4718596
  300.6 8.0 %slice-start = ((s8[12582912]{0:T(1024)(128)(4,1)}), s8[4194304]{0:T(1024)(128)(4,1)S(1)}, s32[]{:S(2)}) async-start(s8[12582912]{0:T(1024)(128)(4,1)} %bitcast.118), calls=%async_computation.14 | async-start | bytes 8388608
  300.6 8.0 %slice-start.1 = ((s8[12582912]{0:T(1024)(128)(4,1)}), s8[4194304]{0:T(1024)(128)(4,1)S(1)}, s32[]{:S(2)}) async-start(s8[12582912]{0:T(1024)(128)(4,1)} %bitcast.118), calls=%async_computation.15 | async-start | bytes 8388608
  304.4 14.6 %copy-start.15 = (bf16[96,8,4,256]{3,1,2,0:T(8,128)(2,1)}, bf16[96,8,4,256]{3,1,2,0:T(8,128)(2,1)S(1)}, u32[]{:S(2)}) copy-start(bf16[96,8,4,256]{3,1,2,0:T(8,128)(2,1)S(1)} %copy.85) | copy-start | bytes 4718596
  323.9 322.9 %all-reduce.8.cloned.1.call-start = ((), (), s32[]{:S(2)}) async-start(), calls=%async_computation.12 | async-start | bytes 9437184
  332.0 34.1 %copy-start.16 = (bf16[96,8,4,256]{3,1,2,0:T(8,128)(2,1)S(1)}, bf16[96,8,4,256]{3,1,2,0:T(8,128)(2,1)}, u32[]{:S(2)}) copy-start(bf16[96,8,4,256]{3,1,2,0:T(8,128)(2,1)} %copy-done.15) | copy-start | bytes 4718596
  332.0 348.6 %all-reduce.10.cloned.1.call-start = ((), (), s32[]{:S(2)}) async-start(), calls=%async_computation.13 | async-start | bytes 1327104 | tf_op jit(solution)/shard_map/psum | solution.py:216
  370.6 100.2 %copy-start.11 = (bf16[1024,768]{1,0:T(8,128)(2,1)S(1)}, bf16[1024,768]{1,0:T(8,128)(2,1)}, u32[]{:S(2)}) copy-start(bf16[1024,768]{1,0:T(8,128)(2,1)} %copy-done.10) | copy-start | bytes 4718596
  370.6 100.2 %copy-start.13 = (bf16[96,8,4,256]{3,1,2,0:T(8,128)(2,1)S(1)}, bf16[96,8,4,256]{3,1,2,0:T(8,128)(2,1)}, u32[]{:S(2)}) copy-start(bf16[96,8,4,256]{3,1,2,0:T(8,128)(2,1)} %copy-done.12) | copy-start | bytes 4718596
  (17 other events, 55.1 us)
Sparse Core Ops, SparseCore 0:
  10.3 50.7 all-gather.6
  63.3 37.0 all-gather.8
  102.8 51.9 all-gather.10
  156.9 51.6 all-gather.12
  256.3 56.7 reduce-scatter.6
  316.9 75.1 reduce-scatter.8
  395.9 74.7 reduce-scatter.10
  474.8 52.3 reduce-scatter.12
  530.9 115.8 all-reduce.7
  649.1 31.5 all-reduce.9
